TPU v7x, 32 devices: a whole 2x2x4 slice. The times are simulated.
32 devices in a mesh: apa: 2 (over y), gz: 4 (over x, core), drift: 4 (over z).
Axes of the slice: x: 2, y: 2, z: 4, core: 2. Of those that a mesh axis runs over, the one named last changes fastest.
Arguments:
- charge: bfloat16 [16384, 384], P(('apa', 'gz', 'drift')), parts along dimension 0, may hold values from 0.049804688 to 2
- intersection: bfloat16 [128, 3, 2, 32, 128], P(('apa', 'gz', 'drift')), parts along dimension 0, may hold values from 0 to 0.03125
- ovl_block: int32 [128, 3, 2], P(('apa', 'gz', 'drift')), parts along dimension 0, may hold values from 0 to 15, as said below
- ovl_count: int32 [128, 3], P(('apa', 'gz', 'drift')), parts along dimension 0, may hold values from 1 to 2
- diff_class: int32 [768], P('apa'), parts along dimension 0, may hold values from 0 to 5
- response: bfloat16 [3, 21, 200], replicated, may hold values from -0.029907227 to 0.029907227
- cotangent: bfloat16 [6, 512, 3072], P('apa', 'gz', 'drift'), parts along dimension 0, may hold values from -120 to 120
Outputs:
- signal: bfloat16 [6, 512, 3072], P('apa', 'gz', 'drift'), parts along dimension 0
- charge_grad: bfloat16 [16384, 384], P(('apa', 'gz', 'drift')), parts along dimension 0
There are 2 independent parts, one for each index of `apa`. A program takes and returns all parts, laid end to end along the dimension named above; an argument that names none is the same for every part. Nothing has to cross between parts.
Inputs may be any that keep to these rules, and one draw needn't show every extreme that they name: `ovl_block`: planes are U, V, W in this order. Cell block b lies in z-block b // 16; its W entries name wire blocks of that z-block, z-block g owning wire blocks g * 4 to (g + 1) * 4 - 1 of every plane. Entry 0 of each list is live. Among the live U and V entries of one group of 4 consecutive cell blocks (starting at a multiple of 4), at most 8 name wire blocks of one z-block, and every such group reaches 8 for some z-block. `ovl_count`: entry k of a list is live where k < count; the others are ignored.
All inputs are finite; a program needn't handle non-finite values.
Results may differ from a plain program's by a relative error of at most 0.0058.
Values may be sent and summed in bfloat16 or wider, within the bound.
A program may use at most 128 MiB of HBM per device.

v0:
```python
import math

import jax
import jax.numpy as jnp
from jax import lax
from jax.sharding import PartitionSpec as P

TPB = 8
HB = 2


def extended_2(cells, sides, width):
    for axis, dim in sides:
        count = lax.axis_size(axis)
        ends = count - 1
        head = lax.slice_in_dim(cells, 0, width, axis=dim)
        tail = lax.slice_in_dim(cells, cells.shape[dim] - width, cells.shape[dim], axis=dim)
        cells = jnp.concatenate(
            [
                lax.ppermute(tail, axis, [(i, (i + 1) % count) for i in range(ends)]),
                cells,
                lax.ppermute(head, axis, [((i + 1) % count, i) for i in range(ends)]),
            ],
            axis=dim,
        )
    return cells


def passed_along(block, axis, distance):
    devices = range(lax.axis_size(axis))
    route = [(i - distance, i) for i in devices if i - distance in devices]
    return lax.ppermute(block, axis, route)


def smear_weights(offset, classes):
    spread_width = TPB * (0.2 + 0.15 * classes)
    reach_ticks = HB * TPB
    samples = jnp.arange(-reach_ticks, reach_ticks).astype(jnp.float32) + 0.5
    normalizer = jnp.sum(
        jnp.exp(-(samples * samples) / (2.0 * spread_width[..., None] * spread_width[..., None])),
        axis=-1,
    )
    inside = jnp.abs(offset) < reach_ticks
    bump = jnp.exp(-(offset * offset) / (2.0 * spread_width * spread_width))
    return jnp.where(inside, bump, jnp.zeros_like(bump)) / normalizer


def windows(padded, count, block_bins):
    length = padded.shape[-1]
    lead = padded.shape[:-1]
    extra = (count + 1) * block_bins - length
    grown = jnp.pad(padded, [(0, 0)] * len(lead) + [(0, extra)])
    front = grown[..., : count * block_bins].reshape(lead + (count, block_bins))
    after = grown[..., block_bins:].reshape(lead + (count, block_bins))[..., : 2 * HB]
    return jnp.concatenate([front, after], axis=-1)


def unwindows(parts, count, block_bins):
    lead = parts.shape[:-2]
    length = count * block_bins + 2 * HB
    front = parts[..., :block_bins].reshape(lead + (count * block_bins,))
    after = jnp.pad(
        parts[..., block_bins:], [(0, 0)] * (len(lead) + 1) + [(0, block_bins - 2 * HB)]
    )
    after = after.reshape(lead + (count * block_bins,))
    front = jnp.pad(front, [(0, 0)] * len(lead) + [(0, 2 * HB)])
    after = jnp.pad(after[..., : length - block_bins], [(0, 0)] * len(lead) + [(block_bins, 0)])
    return front + after


def block_kernel(class_windows, block_bins):
    index_in = jnp.arange(block_bins + 2 * HB).astype(jnp.float32)[:, None]
    tick_in = jnp.arange(block_bins * TPB).astype(jnp.float32)[None, :]
    offset = tick_in - TPB * (index_in - HB) - (TPB - 1) / 2.0
    return smear_weights(offset[None], class_windows[:, :, None])


def drift_forward(framed, class_ext, count, block_bins):
    kernel = block_kernel(windows(class_ext, count, block_bins), block_bins)
    spread = jnp.einsum(
        "pwbi,bit->pwbt",
        windows(framed, count, block_bins),
        kernel,
        precision=lax.Precision.HIGHEST,
    )
    return spread.reshape(spread.shape[0], spread.shape[1], -1)


def drift_backward(tick_values, class_ext, count, block_bins):
    kernel = block_kernel(windows(class_ext, count, block_bins), block_bins)
    framed = tick_values.reshape(tick_values.shape[0], tick_values.shape[1], count, -1)
    parts = jnp.einsum(
        "pwbt,bit->pwbi", framed.astype(jnp.float32), kernel, precision=lax.Precision.HIGHEST
    )
    return unwindows(parts, count, block_bins)


def tick_table(taps, tick_block, forward):
    resp_length = taps.shape[2]
    inputs = jnp.arange(tick_block + resp_length - 1, dtype=jnp.int32)[:, None]
    outputs = jnp.arange(tick_block, dtype=jnp.int32)[None, :]
    if forward:
        lag = outputs + resp_length - 1 - inputs
    else:
        lag = inputs - outputs
    valid = (lag >= 0) & (lag < resp_length)
    picked = taps[:, :, jnp.clip(lag, 0, resp_length - 1)]
    return jnp.where(valid[None, None], picked, jnp.zeros((), taps.dtype))


def planes_apply(extended, taps, wires_here, ticks_here, forward):
    wire_taps, resp_length = (taps.shape[1], taps.shape[2])
    tick_block = math.gcd(ticks_here, 128)
    count = ticks_here // tick_block
    table = tick_table(taps, tick_block, forward)
    shifted = jnp.stack(
        [extended[:, offset : offset + wires_here] for offset in range(wire_taps)], 1
    )
    framed = jnp.stack(
        [
            shifted[..., start * tick_block : start * tick_block + tick_block + resp_length - 1]
            for start in range(count)
        ],
        3,
    )
    result = jnp.einsum("pjwbi,pjit->pwbt", framed, table, preferred_element_type=jnp.float32)
    return result.reshape(result.shape[0], wires_here, ticks_here)


def local(charge, intersection, ovl_block, ovl_count, diff_class, response, cotangent):
    block_count, plane_count, entry_count, wire_block, cell_block = intersection.shape
    bin_count = charge.shape[1]
    owners_total = lax.axis_size("gz")
    z_index = lax.axis_index("gz")
    slab_total = lax.axis_size("drift")
    slab_index = lax.axis_index("drift")
    wires_here = cotangent.shape[1]
    ticks_here = cotangent.shape[2]
    per_owner = wires_here // wire_block
    capacity = 8 * block_count // owners_total
    half_width = (response.shape[1] - 1) // 2
    resp_length = response.shape[2]
    bins_here = bin_count // slab_total
    block_bins = math.gcd(bins_here, 16)
    row_width = wire_block * bin_count
    entry_live = jnp.arange(entry_count, dtype=jnp.int32)[None, None, :] < ovl_count[:, :, None]
    pieces = jnp.einsum(
        "bmc,bcx->bmx",
        intersection.reshape(block_count, plane_count * entry_count * wire_block, cell_block),
        charge.reshape(block_count, cell_block, bin_count),
        preferred_element_type=jnp.float32,
    )
    pieces = pieces.astype(jnp.bfloat16).reshape(block_count, plane_count, entry_count, row_width)
    local_index = ovl_block[:, 2, :].reshape(-1) - z_index * per_owner
    local_pick = (
        (local_index[None, :] == jnp.arange(per_owner)[:, None])
        & entry_live[:, 2, :].reshape(-1)[None, :]
    ).astype(jnp.bfloat16)
    local_sum = jnp.dot(
        local_pick, pieces[:, 2].reshape(-1, row_width), preferred_element_type=jnp.float32
    )
    cross_ids = ovl_block[:, :2, :].reshape(-1)
    cross_live = entry_live[:, :2, :].reshape(-1)
    cross_owner = cross_ids // per_owner
    owner_match = (
        (cross_owner[:, None] == jnp.arange(owners_total)[None, :]) & cross_live[:, None]
    ).astype(jnp.int32)
    earlier_count = jnp.cumsum(owner_match, axis=0) - owner_match
    slot_index = jnp.where(
        cross_live, cross_owner * capacity + jnp.sum(earlier_count * owner_match, axis=1), -1
    )
    slot_pick = (jnp.arange(owners_total * capacity)[:, None] == slot_index[None, :]).astype(
        jnp.bfloat16
    )
    cross_plane = jnp.broadcast_to(
        jnp.arange(2)[None, :, None], (block_count, 2, entry_count)
    ).reshape(-1)
    labels = jnp.where(
        cross_live, cross_plane * per_owner + cross_ids - cross_owner * per_owner + 1, 0
    )
    payload = jnp.dot(
        slot_pick, pieces[:, :2].reshape(-1, row_width), preferred_element_type=jnp.float32
    ).astype(jnp.bfloat16)
    slot_labels = jnp.dot(
        slot_pick, labels.astype(jnp.bfloat16)[:, None], preferred_element_type=jnp.float32
    ).astype(jnp.bfloat16)
    received, received_labels = (
        lax.all_to_all(
            payload.reshape(owners_total, capacity, row_width),
            "gz",
            split_axis=0,
            concat_axis=0,
            tiled=True,
        ),
        lax.all_to_all(
            slot_labels.reshape(owners_total, capacity),
            "gz",
            split_axis=0,
            concat_axis=0,
            tiled=True,
        ),
    )
    arrival = received_labels.reshape(-1).astype(jnp.int32) - 1
    arrival_pick = (jnp.arange(2 * per_owner)[:, None] == arrival[None, :]).astype(jnp.bfloat16)
    cross_sum = jnp.dot(
        arrival_pick, received.reshape(-1, row_width), preferred_element_type=jnp.float32
    )
    currents = jnp.concatenate([cross_sum, local_sum], 0).reshape(
        plane_count, wires_here, bin_count
    )
    class_padded = jnp.pad(diff_class.astype(jnp.float32), (HB, HB), mode="edge")
    class_local = lax.dynamic_slice_in_dim(class_padded, slab_index * bins_here, bins_here + 2 * HB)
    own_bins = lax.psum_scatter(currents, "drift", scatter_dimension=2, tiled=True)
    framed = extended_2(own_bins, (("drift", 2),), HB)
    drifted = drift_forward(framed, class_local, bins_here // block_bins, block_bins).astype(
        jnp.bfloat16
    )
    earlier = passed_along(drifted[:, :, ticks_here - (resp_length - 1) :], "drift", 1)
    extended = extended_2(jnp.concatenate([earlier, drifted], 2), (("gz", 1),), half_width)
    signal = planes_apply(extended, response, wires_here, ticks_here, True).astype(jnp.bfloat16)
    later = passed_along(cotangent[:, :, : resp_length - 1], "drift", -1)
    extended_back = extended_2(jnp.concatenate([cotangent, later], 2), (("gz", 1),), half_width)
    back_ticks = planes_apply(
        extended_back, response[:, ::-1, :], wires_here, ticks_here, False
    ).astype(jnp.bfloat16)
    spread_back = drift_backward(back_ticks, class_local, bins_here // block_bins, block_bins)
    edges = jnp.concatenate([spread_back[:, :, :HB], spread_back[:, :, -HB:]], 2)
    beside_all = extended_2(edges, (("drift", 2),), HB)
    inner = spread_back[:, :, HB : HB + bins_here]
    inner = inner.at[:, :, :HB].add(beside_all[:, :, :HB])
    inner = inner.at[:, :, bins_here - HB :].add(beside_all[:, :, 3 * HB :])
    bin_grads = lax.all_gather(inner.astype(jnp.bfloat16), "drift", axis=2, tiled=True)
    every = lax.all_gather(bin_grads, "gz", axis=1, tiled=True)
    every_rows = every.reshape(plane_count * per_owner * owners_total, row_width)
    plane_base = jnp.arange(plane_count, dtype=jnp.int32)[None, :, None] * (
        per_owner * owners_total
    )
    chosen = jnp.take(every_rows, (plane_base + ovl_block).reshape(-1), axis=0)
    chosen = jnp.where(entry_live.reshape(-1)[:, None], chosen, jnp.zeros((), jnp.bfloat16))
    chosen = chosen.reshape(block_count, plane_count * entry_count * wire_block, bin_count)
    charge_grad = jnp.einsum(
        "bmc,bmx->bcx",
        intersection.reshape(block_count, plane_count * entry_count * wire_block, cell_block),
        chosen,
        preferred_element_type=jnp.float32,
    )
    return (signal, charge_grad.reshape(block_count * cell_block, bin_count).astype(jnp.bfloat16))


def solution(mesh):
    return jax.shard_map(
        local,
        mesh=mesh,
        in_specs=(
            P(("apa", "gz", "drift"), None),
            P(("apa", "gz", "drift"), None, None, None, None),
            P(("apa", "gz", "drift"), None, None),
            P(("apa", "gz", "drift"), None),
            P("apa"),
            P(),
            P("apa", "gz", "drift"),
        ),
        out_specs=(P("apa", "gz", "drift"), P(("apa", "gz", "drift"), None)),
        check_vma=False,
    )
```

profile of v0, /device:TPU:10, one launch (start us, length us, event | category | flops | bytes accessed | tf_op | source)
XLA Modules:
  0.0 491.9 jit_solution(2786146220478637108)
XLA Ops:
  8.0 1.4 copy.280
  9.5 2.4 collective-permute-start.5
  14.9 3.3 all-to-all-start
  19.4 1.2 convolution_convert_fusion.2
  21.3 1.0 copy.275
  22.3 0.9 rev.3
  23.2 111.1 %gather_fusion.1 = bf16[41856,3,21]{2,1,0:T(4,128)(2,1)} fusion(bf16[3,21,200]{1,0,2:T(4,128)(2,1)S(1)} %rev.3, s32[41984]{0:T(1024)S(1)} %get-tuple-element.54), kind=kCustom, calls=%fused_computation.1 | custom fusion | bytes 10715136 | tf_op jit(solution)/shard_map/gather | solution.py:107
  134.4 40.2 %copy.306 = bf16[327,128,3,21]{1,0,3,2:T(8,128)(2,1)} copy(bf16[327,128,3,21]{3,2,1,0:T(4,128)(2,1)} %bitcast.397) | data formatting | bytes 10547712 | tf_op jit(solution)/shard_map/gather | solution.py:107
  177.6 1.3 fusion
  180.0 111.1 %gather_fusion = bf16[41856,3,21]{2,1,0:T(4,128)(2,1)} fusion(bf16[3,21,200]{1,0,2:T(4,128)(2,1)S(1)} %copy.275, s32[41984]{0:T(1024)S(1)} %get-tuple-element.55), kind=kCustom, calls=%fused_computation | custom fusion | bytes 10715136 | tf_op jit(solution)/shard_map/gather | solution.py:107
  291.2 40.2 %copy.276 = bf16[327,128,3,21]{1,0,3,2:T(8,128)(2,1)} copy(bf16[327,128,3,21]{3,2,1,0:T(4,128)(2,1)} %bitcast.398) | data formatting | bytes 10547712 | tf_op jit(solution)/shard_map/gather | solution.py:107
  331.5 0.9 fusion.133
  333.6 2.0 collective-permute-start.6
  336.0 3.5 collective-permute-start.7
  339.6 3.5 all-to-all-start.1
  344.2 1.0 pad_maximum_fusion.1
  352.8 2.7 fusion.6
  355.5 2.7 fusion.5
  358.3 2.7 fusion.4
  361.0 2.6 fusion.3
  363.6 2.7 fusion.2
  366.3 2.7 fusion.1
  369.5 1.1 copy.242
  370.9 17.9 %fusion.29 = bf16[3,128,6,128]{3,1,0,2:T(8,128)(2,1)S(1)} fusion(bf16[3,21,128,6,327]{2,4,1,0,3:T(8,128)(2,1)} %fusion.1, bf16[327,128,3,21]{1,0,3,2:T(8,128)(2,1)} %copy.306, pred[327,128]{1,0:T(8,128)(4,1)S(1)} %fusion.101), kind=kOutput, calls=%fused_computation.47 | convolution fusion | flops 4053253120 | bytes 37548672 | tf_op jit(solution)/shard_map/pjwbi,pjit->pwbt/dot_general | solution.py:126
  389.7 3.9 collective-permute-start.8
  394.4 3.5 collective-permute-start
  397.9 2.4 collective-permute-start.1
  400.3 1.9 collective-permute-start.9
  402.2 1.2 collective-permute-done.1
  403.4 1.0 pad_maximum_fusion.6
  404.4 1.3 fusion.35
  405.8 2.8 collective-permute-start.2
  408.6 4.3 collective-permute-done.2
  413.7 1.9 collective-permute-start.3
  416.1 3.6 collective-permute-start.4
  419.7 14.9 %all_gather.6 = bf16[3,128,384]{1,2,0:T(8,128)(2,1)} all-gather(bf16[3,128,96]{1,2,0:T(8,128)(2,1)S(1)} %convert_element_type.119), channel_id=1, replica_groups=mesh['apa'=2,'gz'=4,'drift'=4] {'drift'}, dimensions={2}, use_global_device_ids=true | all-gather | bytes 368640 | tf_op jit(solution)/shard_map/all_gather | solution.py:232
  435.4 1.1 pad_maximum_fusion
  444.2 3.2 fusion.12
  447.5 3.2 fusion.11
  450.7 3.4 fusion.10
  454.1 3.5 fusion.9
  457.6 3.3 fusion.8
  460.9 3.2 fusion.7
  464.1 14.2 %fusion.32 = bf16[3,128,6,128]{1,3,2,0:T(8,128)(2,1)S(1)} fusion(bf16[3,21,128,6,327]{2,4,1,3,0:T(8,128)(2,1)} %fusion.7, bf16[327,128,3,21]{1,0,3,2:T(8,128)(2,1)} %copy.276, pred[327,128]{1,0:T(8,128)(4,1)S(1)} %fusion.100), kind=kOutput, calls=%fused_computation.48 | convolution fusion | flops 4053253120 | bytes 37548672 | tf_op jit(solution)/shard_map/pjwbi,pjit->pwbt/dot_general | solution.py:126
  478.3 1.1 copy.311
  479.4 1.7 copy.309
  481.7 0.9 gather_fusion.2
  482.9 1.3 convolution_convert_fusion.3
  (167 shorter events, 32.5 us)
Async XLA Ops:
  8.0 11.4 %copy-start = (bf16[512,384]{1,0:T(8,128)(2,1)S(1)}, bf16[512,384]{1,0:T(8,128)(2,1)}, u32[]{:S(2)}) copy-start(bf16[512,384]{1,0:T(8,128)(2,1)} %param.11) | copy-start | bytes 1179652
  9.5 323.4 %collective-permute-start.5 = (bf16[3,128,199]{1,2,0:T(8,128)(2,1)S(1)}, bf16[3,128,199]{1,2,0:T(8,128)(2,1)S(1)}, u32[]{:S(2)}, u32[]{:S(2)}) collective-permute-start(bf16[3,128,199]{1,2,0:T(8,128)(2,1)S(1)} %slice.477), channel_id=1, source_target_pairs={{1,0},{2,1},{3,2},{5,4},{6,5},{7,6},{9,8},{10,9},{11,10},{13,12},{... | collective-permute-start | bytes 458504 | tf_op jit(solution)/shard_map/ppermute | solution.py:32
  14.9 324.6 %all-to-all-start = ((bf16[4,1,8]{2,1,0:T(2,128)(2,1)}), bf16[4,1,8]{2,1,0:T(2,128)(2,1)S(1)}, u32[]{:S(2)}, u32[]{:S(2)}) async-start(bf16[4,1,8]{2,1,0:T(2,128)(2,1)} %all_to_all.12), calls=%async_computation | async-start | bytes 4096 | tf_op jit(solution)/shard_map/all_to_all | solution.py:195
  134.4 40.2 %copy-start.4 = (s32[384]{0:T(512)S(1)}, s32[384]{0:T(512)}, u32[]{:S(2)}) copy-start(s32[384]{0:T(512)} %param.15) | copy-start | bytes 4612
  333.6 9.8 %collective-permute-start.6 = (bf16[3,10,967]{2,0,1:T(4,128)(2,1)S(1)}, bf16[3,10,967]{2,0,1:T(4,128)(2,1)S(1)}, u32[]{:S(2)}, u32[]{:S(2)}) collective-permute-start(bf16[3,10,967]{2,0,1:T(4,128)(2,1)S(1)} %copy.281), channel_id=1, source_target_pairs={{0,4},{4,8},{8,12},{1,5},{5,9},{9,13},{2,6},{6,10},{10,14},{3,7},{... | collective-permute-start | bytes 174068 | tf_op jit(solution)/shard_map/ppermute | solution.py:20
  336.0 7.8 %collective-permute-start.7 = (bf16[3,10,967]{2,0,1:T(4,128)(2,1)S(1)}, bf16[3,10,967]{2,0,1:T(4,128)(2,1)S(1)}, u32[]{:S(2)}, u32[]{:S(2)}) collective-permute-start(bf16[3,10,967]{2,0,1:T(4,128)(2,1)S(1)} %copy.283), channel_id=1, source_target_pairs={{4,0},{8,4},{12,8},{5,1},{9,5},{13,9},{6,2},{10,6},{14,10},{7,3},{... | collective-permute-start | bytes 174068 | tf_op jit(solution)/shard_map/ppermute | solution.py:22
  339.6 29.5 %all-to-all-start.1 = ((bf16[4,8,12288]{2,1,0:T(8,128)(2,1)}), bf16[4,8,12288]{2,1,0:T(8,128)(2,1)S(1)}, u32[]{:S(2)}, u32[]{:S(2)}) async-start(bf16[4,8,12288]{2,1,0:T(8,128)(2,1)} %fusion), calls=%async_computation.1 | async-start | bytes 1572864 | tf_op jit(solution)/shard_map/all_to_all | solution.py:188
  343.1 50.6 %reduce-scatter.2.cloned.1.call-start = ((), (), s32[]{:S(2)}) async-start(), calls=%async_computation.3 | async-start | bytes 737280 | tf_op jit(solution)/shard_map/reduce_scatter | solution.py:213
  361.0 8.3 %copy-start.2 = (f32[4,12288]{1,0:T(4,128)S(1)}, f32[4,12288]{1,0:T(4,128)}, u32[]{:S(2)}) copy-start(f32[4,12288]{1,0:T(4,128)} %fusion.133) | copy-start | bytes 589828
  370.6 108.8 %all-gather.2.cloned.1.call-start = ((), (), s32[]{:S(2)}) async-start(), calls=%async_computation.4 | async-start | bytes 1474560 | tf_op jit(solution)/shard_map/all_gather | solution.py:233
  389.7 10.6 %collective-permute-start.8 = (f32[3,128,2]{1,2,0:T(2,128)S(1)}, f32[3,128,2]{1,2,0:T(2,128)S(1)}, u32[]{:S(2)}, u32[]{:S(2)}) collective-permute-start(f32[3,128,2]{1,2,0:T(2,128)S(1)} %fusion.126), channel_id=1, source_target_pairs={{0,1},{1,2},{2,3},{4,5},{5,6},{6,7},{8,9},{9,10},{10,11},{12,13},{... | collective-permute-start | bytes 9224 | tf_op jit(solution)/shard_map/ppermute | solution.py:20
  394.4 7.8 %collective-permute-start = (f32[3,128,2]{1,2,0:T(2,128)S(1)}, f32[3,128,2]{1,2,0:T(2,128)S(1)}, u32[]{:S(2)}, u32[]{:S(2)}) collective-permute-start(f32[3,128,2]{1,2,0:T(2,128)S(1)} %get-tuple-element.48), channel_id=1, source_target_pairs={{0,1},{1,2},{2,3},{4,5},{5,6},{6,7},{8,9},{9,10},{10,11},{12,13},{... | collective-permute-start | bytes 9224 | tf_op jit(solution)/shard_map/ppermute | solution.py:20
  397.9 5.5 %collective-permute-start.1 = (f32[3,128,2]{1,2,0:T(2,128)S(1)}, f32[3,128,2]{1,2,0:T(2,128)S(1)}, u32[]{:S(2)}, u32[]{:S(2)}) collective-permute-start(f32[3,128,2]{1,2,0:T(2,128)S(1)} %get-tuple-element.49), channel_id=1, source_target_pairs={{1,0},{2,1},{3,2},{5,4},{6,5},{7,6},{9,8},{10,9},{11,10},{13,12},{... | collective-permute-start | bytes 9224 | tf_op jit(solution)/shard_map/ppermute | solution.py:22
  400.3 8.3 %collective-permute-start.9 = (f32[3,128,2]{1,2,0:T(2,128)S(1)}, f32[3,128,2]{1,2,0:T(2,128)S(1)}, u32[]{:S(2)}, u32[]{:S(2)}) collective-permute-start(f32[3,128,2]{1,2,0:T(2,128)S(1)} %get-tuple-element.44), channel_id=1, source_target_pairs={{1,0},{2,1},{3,2},{5,4},{6,5},{7,6},{9,8},{10,9},{11,10},{13,12},{... | collective-permute-start | bytes 9224 | tf_op jit(solution)/shard_map/ppermute | solution.py:22
  405.8 7.1 %collective-permute-start.2 = (bf16[3,128,199]{1,2,0:T(8,128)(2,1)S(1)}, bf16[3,128,199]{1,2,0:T(8,128)(2,1)S(1)}, u32[]{:S(2)}, u32[]{:S(2)}) collective-permute-start(bf16[3,128,199]{1,2,0:T(8,128)(2,1)S(1)} %slice.446), channel_id=1, source_target_pairs={{0,1},{1,2},{2,3},{4,5},{5,6},{6,7},{8,9},{9,10},{10,11},{12,13},{... | collective-permute-start | bytes 458504 | tf_op jit(solution)/shard_map/ppermute | solution.py:32
  413.7 20.9 %collective-permute-start.3 = (bf16[3,10,967]{2,0,1:T(4,128)(2,1)S(1)}, bf16[3,10,967]{2,0,1:T(4,128)(2,1)S(1)}, u32[]{:S(2)}, u32[]{:S(2)}) collective-permute-start(bf16[3,10,967]{2,0,1:T(4,128)(2,1)S(1)} %copy.246), channel_id=1, source_target_pairs={{0,4},{4,8},{8,12},{1,5},{5,9},{9,13},{2,6},{6,10},{10,14},{3,7},{... | collective-permute-start | bytes 174068 | tf_op jit(solution)/shard_map/ppermute | solution.py:20
  416.1 19.0 %collective-permute-start.4 = (bf16[3,10,967]{2,0,1:T(4,128)(2,1)S(1)}, bf16[3,10,967]{2,0,1:T(4,128)(2,1)S(1)}, u32[]{:S(2)}, u32[]{:S(2)}) collective-permute-start(bf16[3,10,967]{2,0,1:T(4,128)(2,1)S(1)} %copy.248), channel_id=1, source_target_pairs={{4,0},{8,4},{12,8},{5,1},{9,5},{13,9},{6,2},{10,6},{14,10},{7,3},{... | collective-permute-start | bytes 174068 | tf_op jit(solution)/shard_map/ppermute | solution.py:22
  464.1 18.8 %copy-start.3 = (bf16[4,3,2,32,128]{4,3,2,1,0:T(8,128)(2,1)S(1)}, bf16[4,3,2,32,128]{4,3,2,1,0:T(8,128)(2,1)}, u32[]{:S(2)}) copy-start(bf16[4,3,2,32,128]{4,3,2,1,0:T(8,128)(2,1)} %param.12) | copy-start | bytes 589828
  464.1 20.1 %copy-start.1 = (bf16[512,384]{1,0:T(8,128)(2,1)S(1)}, bf16[512,384]{1,0:T(8,128)(2,1)}, u32[]{:S(2)}) copy-start(bf16[512,384]{1,0:T(8,128)(2,1)} %param.11) | copy-start | bytes 1179652
Sparse Core Ops, SparseCore 0:
  370.7 20.9 reduce-scatter.1
Sparse Core Ops, SparseCore 1:
  434.7 17.5 all-gather.1
where the time goes:
time: 500 us; the launch traced here: 492 us
  local copies, waits for them, and re-layouts  374 us (75%)
  matrix products  39.2 us (8%)
  starting transfers between devices  35.2 us (7%)
  between operations  16.5 us (3%)
  blocking collectives  14.9 us (3%)
  other arithmetic  7.02 us (1%)
  waiting for transfers between devices  5.52 us (1%)
    gather x4, local copies, waits for them, and re-layouts, tick_table(): picked = taps[:, :, jnp.clip(lag, 0, resp_length - 1)]  303 us
    unnamed x63, local copies, waits for them, and re-layouts  48.5 us
    dot_general x2, matrix products, planes_apply(): jnp.einsum('pjwbi,pjit->pwbt', framed, table, preferred_element_type=jnp....  32.1 us
    all_gather x1, blocking collectives, local(): lax.all_gather(inner.astype(jnp.bfloat16), 'drift', axis=2, tiled=True)  14.9 us
    ppermute x4, starting transfers between devices, extended_2(): lax.ppermute(head, axis, [((i + 1) % count, i) for i in range(ends)])  11.4 us
    ppermute x4, starting transfers between devices, extended_2(): lax.ppermute(tail, axis, [(i, (i + 1) % count) for i in range(ends)])  11.3 us
  transfers between devices with their start and end apart: 14, of which 2 were waited for; matrix products, arithmetic and copies ran while one was open for 83% of the time, Pallas kernels for 0%

commit v1 on v0

v1 whole, which is shorter than its diff:
```python
import functools
import math

import jax
import jax.numpy as jnp
from jax import lax
from jax.experimental import pallas as pl
from jax.experimental.pallas import tpu as pltpu
from jax.sharding import PartitionSpec as P


TPB = 8
HB = 2
LANES = 128
ROWS = 16

VMEM = pl.BlockSpec(memory_space=pltpu.VMEM)
SMEM = pl.BlockSpec(memory_space=pltpu.SMEM)


def round_up(value, step):
    return -(-value // step) * step


def iota(shape, dim):
    return lax.broadcasted_iota(jnp.int32, shape, dim)


def smear_weights(offset, classes):
    width = TPB * (0.2 + 0.15 * classes)
    reach = HB * TPB
    scale = 1.0 / (2.0 * width * width)
    normalizer = jnp.zeros_like(width)
    for j in range(-reach, reach):
        normalizer += jnp.exp(-((j + 0.5) ** 2) * scale)
    bump = jnp.exp(-(offset * offset) * scale)
    return jnp.where(jnp.abs(offset) < reach, bump, 0.0) / normalizer


def split_dot(left, right, dims):
    return lax.dot_general(
        left.astype(jnp.float32),
        right,
        (dims, ((), ())),
        precision=lax.Precision.HIGHEST,
        preferred_element_type=jnp.float32,
    )


def pieces_kernel(dims, blk_ref, count_ref, charge_ref, inter_ref, pay_ref, own_ref, seen_ref):
    owners, slabs, per_owner, capacity, bins_here, front, width, used = dims
    blocks, rows, cells = inter_ref.shape
    entries, wires = 2, rows // 6
    bins = charge_ref.shape[1]
    z_index = lax.axis_index("gz")
    x = iota((bins, slabs * width), 0)
    lane = iota((bins, slabs * width), 1)
    place = jnp.where(
        (x == (lane // width) * bins_here - front + lane % width) & (lane % width < used), 1.0, 0.0
    ).astype(jnp.bfloat16)
    pay_ref[...] = jnp.zeros_like(pay_ref)
    own_ref[...] = jnp.zeros_like(own_ref)
    for g in range(owners):
        seen_ref[g] = 0
    is_label = iota((wires, width), 1) == width - 1
    for b in range(blocks):
        framed = jnp.dot(
            charge_ref[b * cells : (b + 1) * cells], place, preferred_element_type=jnp.float32
        ).astype(jnp.bfloat16)
        piece = jnp.dot(inter_ref[b], framed, preferred_element_type=jnp.float32)
        piece = piece.astype(jnp.bfloat16).astype(jnp.float32)
        for p in range(3):
            for k in range(entries):
                e = (b * 3 + p) * entries + k
                block = blk_ref[e]
                row = (p * entries + k) * wires
                mine = piece[row : row + wires]

                @pl.when(k < count_ref[b * 3 + p])
                def _():
                    if p == 2:
                        at = pl.multiple_of((block - z_index * per_owner) * wires, wires)
                        for d in range(slabs):
                            own_ref[d, pl.ds(at, wires), :] += mine[:, d * width : (d + 1) * width]
                    else:
                        owner = block // per_owner
                        slot = seen_ref[owner]
                        seen_ref[owner] = slot + 1
                        label = (p * per_owner + block - owner * per_owner + 1).astype(jnp.float32)
                        for d in range(slabs):
                            part = jnp.where(is_label, label, mine[:, d * width : (d + 1) * width])
                            pay_ref[(owner * slabs + d) * capacity + slot] = part.astype(
                                jnp.bfloat16
                            )


def drift_kernel(dims, recv_ref, own_ref, class_ref, out_ref):
    per_owner, wires, width, _, front, lead, ticks_here = dims
    total = out_ref.shape[2]
    slab = lax.axis_index("drift")
    unroll = math.gcd(recv_ref.shape[0], 4)

    def add(step, sums):
        for u in range(unroll):
            part = recv_ref[step * unroll + u].astype(jnp.float32)
            label = part[:, width - 1 : width]
            sums = tuple(s + jnp.where(label == q + 1, part, 0.0) for q, s in enumerate(sums))
        return sums

    zero = jnp.zeros((wires, width), jnp.float32)
    sums = lax.fori_loop(0, recv_ref.shape[0] // unroll, add, (zero,) * (2 * per_owner))
    own = own_ref[0]
    for d in range(1, own_ref.shape[0]):
        own = own + own_ref[d]
    tick = iota((width, total), 1) - lead
    offset = (tick - TPB * (iota((width, total), 0) - front)).astype(jnp.float32) - (TPB - 1) / 2
    weights = smear_weights(offset, class_ref[...])
    weights = jnp.where(tick + slab * ticks_here >= 0, weights, 0.0)
    currents = jnp.concatenate(list(sums) + [own], 0)
    currents = jnp.where(iota(currents.shape, 1) == width - 1, 0.0, currents)
    drifted = split_dot(currents, weights, ((1,), (0,))).astype(jnp.bfloat16)
    here = per_owner * wires
    for p in range(3):
        out_ref[p] = drifted[p * here : (p + 1) * here]


def convolve(main_ref, prev_ref, next_ref, taps_ref, ext_ref, acc_ref, block, depth, first):
    here = main_ref.shape[1]
    count = acc_ref.shape[0] // here
    ext_ref[:ROWS] = prev_ref[0].astype(jnp.float32)
    ext_ref[ROWS : ROWS + here] = main_ref[0].astype(jnp.float32)
    ext_ref[ROWS + here :] = next_ref[0].astype(jnp.float32)
    acc_ref[...] = jnp.zeros_like(acc_ref)

    for j in range(taps_ref.shape[1]):
        shifted = ext_ref[first + j : first + j + here, :].astype(jnp.bfloat16)
        row = jnp.broadcast_to(taps_ref[0, j : j + 1, :], (block, depth))
        table = pltpu.roll(row, 0, 1, stride=1, stride_axis=0).astype(jnp.bfloat16)
        framed = jnp.concatenate(
            [shifted[:, c * block : c * block + depth] for c in range(count)], 0
        )
        acc_ref[...] += lax.dot_general(
            framed, table, (((1,), (1,)), ((), ())), preferred_element_type=jnp.float32
        )


def signal_kernel(dims, main_ref, prev_ref, next_ref, taps_ref, out_ref, ext_ref, acc_ref):
    block, depth, first = dims
    convolve(main_ref, prev_ref, next_ref, taps_ref, ext_ref, acc_ref, block, depth, first)
    here = main_ref.shape[1]
    for c in range(acc_ref.shape[0] // here):
        out_ref[0, :, c * block : (c + 1) * block] = acc_ref[c * here : (c + 1) * here].astype(
            jnp.bfloat16
        )


def bins_kernel(
    dims, main_ref, prev_ref, next_ref, taps_ref, class_ref, out_ref, ext_ref, acc_ref
):
    block, depth, first = dims
    convolve(main_ref, prev_ref, next_ref, taps_ref, ext_ref, acc_ref, block, depth, first)
    here = main_ref.shape[1]
    total = jnp.zeros(out_ref.shape[1:], jnp.float32)
    shape = (block, out_ref.shape[2])
    for c in range(acc_ref.shape[0] // here):
        ticks = acc_ref[c * here : (c + 1) * here].astype(jnp.bfloat16)
        offset = c * block + iota(shape, 0) - TPB * (iota(shape, 1) - HB)
        weights = smear_weights(offset.astype(jnp.float32) - (TPB - 1) / 2, class_ref[...])
        total += split_dot(ticks, weights, ((1,), (0,)))
    out_ref[0] = total.astype(jnp.bfloat16)


def grads_kernel(dims, blk_ref, count_ref, every_ref, inter_ref, out_ref, pick_ref):
    slabs, per_owner, bins_here, width = dims
    blocks, rows, cells = inter_ref.shape
    entries, wires = 2, rows // 6
    bins = out_ref.shape[1]
    lane = iota((slabs * width, bins), 0)
    x = iota((slabs * width, bins), 1)
    place = jnp.where(
        (x == (lane // width) * bins_here - HB + lane % width)
        & (lane % width < bins_here + 2 * HB),
        1.0,
        0.0,
    ).astype(jnp.bfloat16)
    for b in range(blocks):
        for p in range(3):
            for k in range(entries):
                block = blk_ref[(b * 3 + p) * entries + k]
                live = k < count_ref[b * 3 + p]
                owner = block // per_owner
                row = (p * entries + k) * wires
                for d in range(slabs):
                    at = ((owner * slabs + d) * 3 + p) * per_owner + block - owner * per_owner
                    part = every_ref[at]
                    pick_ref[row : row + wires, d * width : (d + 1) * width] = jnp.where(
                        live, part, jnp.zeros_like(part)
                    )
        chosen = jnp.dot(pick_ref[...], place, preferred_element_type=jnp.float32)
        out_ref[b * cells : (b + 1) * cells] = lax.dot_general(
            inter_ref[b],
            chosen.astype(jnp.bfloat16),
            (((0,), (0,)), ((), ())),
            preferred_element_type=jnp.float32,
        ).astype(jnp.bfloat16)


def moved(block, axis, distance):
    devices = range(lax.axis_size(axis))
    return lax.ppermute(
        block, axis, [(i - distance, i) for i in devices if i - distance in devices]
    )


def local(charge, intersection, ovl_block, ovl_count, diff_class, response, cotangent):
    blocks, planes, entries, wires, cells = intersection.shape
    bins = charge.shape[1]
    owners, slabs = lax.axis_size("gz"), lax.axis_size("drift")
    slab = lax.axis_index("drift")
    here, ticks_here = cotangent.shape[1:]
    per_owner = here // wires
    capacity = 8 * blocks // owners
    spread, length = response.shape[1:]
    half = (spread - 1) // 2
    first = ROWS - half
    bins_here = bins // slabs
    front = (length - 1 + HB * TPB + (TPB - 1) // 2) // TPB
    used = front + bins_here + HB
    width = round_up(used + 1, LANES)
    grad_width = round_up(bins_here + 2 * HB, LANES)
    block = math.gcd(ticks_here, 256)
    depth = round_up(block + length - 1, LANES)
    lead = depth - block
    total = ticks_here + lead
    count = ticks_here // block

    inter = intersection.reshape(blocks, planes * entries * wires, cells)
    blk = ovl_block.reshape(-1)
    cnt = ovl_count.reshape(-1)
    classes = diff_class.astype(jnp.float32)

    def class_window(lo, n):
        padded = jnp.pad(classes, (LANES * 2, LANES * 2), mode="edge")
        return lax.dynamic_slice_in_dim(padded, slab * bins_here - lo + LANES * 2, n)

    taps = response.astype(jnp.float32)
    forward_taps = jnp.pad(
        taps[:, :, ::-1], ((0, 0), (0, 0), (lead - length + 1, depth - lead - 1))
    )
    backward_taps = jnp.pad(taps[:, ::-1, :], ((0, 0), (0, 0), (0, depth - length)))

    payload, own = pl.pallas_call(
        functools.partial(
            pieces_kernel,
            (owners, slabs, per_owner, capacity, bins_here, front, width, used),
        ),
        out_shape=(
            jax.ShapeDtypeStruct((owners * slabs * capacity, wires, width), jnp.bfloat16),
            jax.ShapeDtypeStruct((slabs, here, width), jnp.float32),
        ),
        in_specs=[SMEM, SMEM, VMEM, VMEM],
        out_specs=(VMEM, VMEM),
        scratch_shapes=[pltpu.SMEM((owners,), jnp.int32)],
        name="pieces",
    )(blk, cnt, charge, inter)

    recv = lax.all_to_all(payload, ("gz", "drift"), 0, 0, tiled=True)
    own_sum = lax.psum_scatter(own, "drift", scatter_dimension=0, tiled=True)

    def plane_spec(rows, columns):
        return pl.BlockSpec((1, rows, columns), lambda p: (p, 0, 0))

    conv_specs = [
        plane_spec(here, total),
        plane_spec(ROWS, total),
        plane_spec(ROWS, total),
        plane_spec(spread, depth),
    ]
    conv_scratch = [
        pltpu.VMEM((here + 2 * ROWS, total), jnp.float32),
        pltpu.VMEM((count * here, block), jnp.float32),
    ]
    conv_cost = pl.CostEstimate(
        flops=2 * planes * spread * here * count * depth * block,
        bytes_accessed=4 * planes * here * total,
        transcendentals=0,
    )

    later = moved(cotangent[:, :, :lead], "drift", -1)
    cot = jnp.concatenate([cotangent, later], 2)
    cot_prev = moved(cot[:, here - ROWS :], "gz", 1)
    cot_next = moved(cot[:, :ROWS], "gz", -1)
    partial_bins = pl.pallas_call(
        functools.partial(bins_kernel, (block, depth, first)),
        grid=(planes,),
        out_shape=jax.ShapeDtypeStruct((planes, here, grad_width), jnp.bfloat16),
        in_specs=conv_specs + [pl.BlockSpec((1, grad_width), lambda p: (0, 0))],
        out_specs=plane_spec(here, grad_width),
        scratch_shapes=conv_scratch,
        cost_estimate=conv_cost,
        name="bins",
    )(cot, cot_prev, cot_next, backward_taps, class_window(HB, grad_width)[None, :])
    every = lax.all_gather(partial_bins, ("gz", "drift"), axis=0, tiled=True)

    drifted = pl.pallas_call(
        functools.partial(
            drift_kernel, (per_owner, wires, width, bins_here, front, lead, ticks_here)
        ),
        out_shape=jax.ShapeDtypeStruct((planes, here, total), jnp.bfloat16),
        in_specs=[VMEM, VMEM, VMEM],
        out_specs=VMEM,
        name="drift",
    )(recv, own_sum, class_window(front, width)[:, None])
    drift_prev = moved(drifted[:, here - ROWS :], "gz", 1)
    drift_next = moved(drifted[:, :ROWS], "gz", -1)
    signal = pl.pallas_call(
        functools.partial(signal_kernel, (block, depth, first)),
        grid=(planes,),
        out_shape=jax.ShapeDtypeStruct((planes, here, ticks_here), jnp.bfloat16),
        in_specs=conv_specs,
        out_specs=plane_spec(here, ticks_here),
        scratch_shapes=conv_scratch,
        cost_estimate=conv_cost,
        name="signal",
    )(drifted, drift_prev, drift_next, forward_taps)

    charge_grad = pl.pallas_call(
        functools.partial(grads_kernel, (slabs, per_owner, bins_here, grad_width)),
        out_shape=jax.ShapeDtypeStruct((blocks * cells, bins), jnp.bfloat16),
        in_specs=[SMEM, SMEM, VMEM, VMEM],
        out_specs=VMEM,
        scratch_shapes=[pltpu.VMEM((planes * entries * wires, slabs * grad_width), jnp.bfloat16)],
        name="grads",
    )(blk, cnt, every.reshape(owners * slabs * planes * per_owner, wires, grad_width), inter)
    return signal, charge_grad


def solution(mesh):
    return jax.shard_map(
        local,
        mesh=mesh,
        in_specs=(
            P(("apa", "gz", "drift"), None),
            P(("apa", "gz", "drift"), None, None, None, None),
            P(("apa", "gz", "drift"), None, None),
            P(("apa", "gz", "drift"), None),
            P("apa"),
            P(),
            P("apa", "gz", "drift"),
        ),
        out_specs=(P("apa", "gz", "drift"), P(("apa", "gz", "drift"), None)),
        check_vma=False,
    )
```

time: 500 us -> 124 us (0.25)
  the two profiles are of different devices: /device:TPU:10 before, /device:TPU:1 now
where the time goes in v1:
time: 124 us
  Pallas kernels  39.3 us (32%)
  waiting for transfers between devices  38.5 us (31%)
  starting transfers between devices  16.8 us (14%)
  between operations  15.6 us (13%)
  local copies, waits for them, and re-layouts  12.7 us (10%)
    all_to_all x1, waiting for transfers between devices, local(): recv = lax.all_to_all(payload, ('gz', 'drift'), 0, 0, tiled=True)  28.6 us
    ppermute x5, starting transfers between devices, moved(): lax.ppermute(block, axis, [(i - distance, i) for i in devices if i - dist...  12.6 us
    pallas_call x1, Pallas kernels, local(): pl.pallas_call(functools.partial(bins_kernel, (block, depth, first)), gri...  12 us
    pallas_call x1, Pallas kernels, local(): pl.pallas_call(functools.partial(drift_kernel, (per_owner, wires, width,...  10.5 us
    ppermute x5, waiting for transfers between devices, moved(): lax.ppermute(block, axis, [(i - distance, i) for i in devices if i - dist...  9.85 us
    pallas_call x1, Pallas kernels, local(): pl.pallas_call(functools.partial(signal_kernel, (block, depth, first)), g...  9.07 us
    pallas_call x1, Pallas kernels, local(): pl.pallas_call(functools.partial(pieces_kernel, (owners, slabs, per_owner...  4.24 us
    all_to_all x1, starting transfers between devices, local(): recv = lax.all_to_all(payload, ('gz', 'drift'), 0, 0, tiled=True)  4.1 us
  transfers between devices with their start and end apart: 8, of which 4 were waited for; matrix products, arithmetic and copies ran while one was open for 7% of the time, Pallas kernels for 26%

profile of v1, /device:TPU:1, one launch (start us, length us, event | category | flops | bytes accessed | tf_op | source)
XLA Modules:
  0.0 123.6 jit_solution(13966154739822864492)
XLA Ops:
  8.0 0.0 copy-start.1
  8.0 0.0 reduce-scatter.2.cloned.1.call-start
  8.1 0.8 copy.13
  8.9 0.6 reshape.28.blk_ref
  9.5 1.3 %reshape.29.count_ref = s32[12]{0:T(128)} reshape(s32[4,3]{1,0:T(4,128)} %param.10) | data formatting | bytes 96 | tf_op jit(solution)/shard_map/reshape | solution.py:239
  10.8 4.2 %pieces.1 = (bf16[128,32,128]{2,1,0:T(8,128)(2,1)}, f32[4,128,128]{2,1,0:T(8,128)}) custom-call(s32[24]{0:T(128)} %reshape.28.blk_ref, s32[12]{0:T(128)} %reshape.29.count_ref, bf16[512,384]{1,0:T(8,128)(2,1)} %charge_ref.1, bf16[4,192,128]{2,1,0:T(8,128)(2,1)} %bitcast.10), custom_call_target="tpu_custom_call" | custom-call | tf_op jit(solution)/shard_map/pieces/pallas_call | solution.py:252
  15.1 0.0 reduce-scatter.2.cloned.1.call-update
  15.1 0.0 all-gather.2.cloned.1.call-start
  15.1 0.9 slice.35
  16.1 1.3 %collective-permute-start.2 = (bf16[3,128,256]{2,1,0:T(8,128)(2,1)S(1)}, bf16[3,128,256]{2,1,0:T(8,128)(2,1)S(1)}, u32[]{:S(2)}, u32[]{:S(2)}) collective-permute-start(bf16[3,128,256]{2,1,0:T(8,128)(2,1)S(1)} %slice.35), channel_id=1, source_target_pairs={{1,0},{2,1},{3,2},{5,4},{6,5},{7,6},{9,8},{10,9},{11,10},{13,12},{... | collective-permute-start | bytes 589832 | tf_op jit(solution)/shard_map/ppermute | solution.py:210
  17.4 0.7 convert_element_type.10
  18.1 0.6 fusion.2
  18.7 0.8 rev.7
  19.5 0.7 pad.9.taps_ref
  20.2 0.6 reshape.31
  20.8 0.6 reshape.32
  21.4 0.0 copy-done.1
  21.4 0.1 constant_dynamic-update-slice_fusion.1
  21.5 3.1 %collective-permute-done.2 = bf16[3,128,256]{2,1,0:T(8,128)(2,1)S(1)} collective-permute-done((bf16[3,128,256]{2,1,0:T(8,128)(2,1)S(1)}, bf16[3,128,256]{2,1,0:T(8,128)(2,1)S(1)}, u32[]{:S(2)}, u32[]{:S(2)}) %collective-permute-start.2) | collective-permute-done | bytes 196640 | tf_op jit(solution)/shard_map/ppermute | solution.py:210
  24.7 0.0 copy-start.2
  24.7 4.6 %collective-permute-start.3 = (bf16[3,16,1024]{2,1,0:T(8,128)(2,1)S(1)}, bf16[3,16,1024]{2,1,0:T(8,128)(2,1)S(1)}, u32[]{:S(2)}, u32[]{:S(2)}) collective-permute-start(bf16[3,16,1024]{2,1,0:T(8,128)(2,1)S(1)} %get-tuple-element.7), channel_id=1, source_target_pairs={{0,4},{4,8},{8,12},{1,5},{5,9},{9,13},{2,6},{6,10},{10,14},{3,7},{... | collective-permute-start | bytes 294920 | tf_op jit(solution)/shard_map/ppermute | solution.py:210
  29.3 1.9 %collective-permute-start.4 = (bf16[3,16,1024]{2,1,0:T(8,128)(2,1)S(1)}, bf16[3,16,1024]{2,1,0:T(8,128)(2,1)S(1)}, u32[]{:S(2)}, u32[]{:S(2)}) collective-permute-start(bf16[3,16,1024]{2,1,0:T(8,128)(2,1)S(1)} %get-tuple-element.6), channel_id=1, source_target_pairs={{4,0},{8,4},{12,8},{5,1},{9,5},{13,9},{6,2},{10,6},{14,10},{7,3},{... | collective-permute-start | bytes 294920 | tf_op jit(solution)/shard_map/ppermute | solution.py:210
  31.3 0.6 dynamic-slice_bitcast_fusion
  31.9 0.0 collective-permute-done.3.prev_ref
  31.9 3.8 %collective-permute-done.4.next_ref = bf16[3,16,1024]{2,1,0:T(8,128)(2,1)S(1)} collective-permute-done((bf16[3,16,1024]{2,1,0:T(8,128)(2,1)S(1)}, bf16[3,16,1024]{2,1,0:T(8,128)(2,1)S(1)}, u32[]{:S(2)}, u32[]{:S(2)}) %collective-permute-start.4) | collective-permute-done | bytes 98336 | tf_op jit(solution)/shard_map/ppermute | solution.py:210
  35.7 0.0 copy-done.2
  35.7 0.0 copy-done.5
  35.7 0.6 copy-done.7
  36.3 12.0 %bins.1 = bf16[3,128,128]{2,1,0:T(8,128)(2,1)} custom-call(bf16[3,128,1024]{2,1,0:T(8,128)(2,1)} %copy-done.2, bf16[3,16,1024]{2,1,0:T(8,128)(2,1)} %copy-done.5, bf16[3,16,1024]{2,1,0:T(8,128)(2,1)} %copy-done.7, f32[3,21,512]{2,1,0:T(8,128)} %pad.9.taps_ref, f32[1,128]{1,0:T(1,128)} %get-tuple-element.10.class_ref), custom_call_target="tpu_custom_call" | custom-call | flops 6341787648 | bytes 1572864 | tf_op jit(solution)/shard_map/bins/pallas_call | solution.py:293
  48.3 0.0 all-gather.2.cloned.1.call-update
  48.3 4.1 %all-to-all-start = ((bf16[128,32,128]{2,1,0:T(8,128)(2,1)}), bf16[128,32,128]{2,1,0:T(8,128)(2,1)S(1)}, u32[]{:S(2)}, u32[]{:S(2)}) async-start(bf16[128,32,128]{2,1,0:T(8,128)(2,1)} %get-tuple-element.4), calls=%async_computation | async-start | bytes 2097152 | tf_op jit(solution)/shard_map/all_to_all | solution.py:267
  52.4 0.7 copy.14.class_ref
  53.2 28.6 %all-to-all-done.recv_ref = bf16[128,32,128]{2,1,0:T(8,128)(2,1)S(1)} async-done(((bf16[128,32,128]{2,1,0:T(8,128)(2,1)}), bf16[128,32,128]{2,1,0:T(8,128)(2,1)S(1)}, u32[]{:S(2)}, u32[]{:S(2)}) %all-to-all-start) | async-done | bytes 1048608 | tf_op jit(solution)/shard_map/all_to_all | solution.py:267
  81.7 1.0 copy-done
  82.7 10.5 %drift.1.main_ref = bf16[3,128,1024]{2,1,0:T(8,128)(2,1)} custom-call(bf16[128,32,128]{2,1,0:T(8,128)(2,1)} %copy-done, f32[1,128,128]{2,1,0:T(8,128)} %reduce-scatter.2.cloned.1.call-done.own_ref, f32[128,1]{1,0:T(8,128)} %copy.14.class_ref), custom_call_target="tpu_custom_call" | custom-call | tf_op jit(solution)/shard_map/drift/pallas_call | solution.py:305
  93.2 1.0 fusion.1
  94.1 2.8 %collective-permute-start = (bf16[3,16,1024]{2,1,0:T(8,128)(2,1)S(1)}, bf16[3,16,1024]{2,1,0:T(8,128)(2,1)S(1)}, u32[]{:S(2)}, u32[]{:S(2)}) collective-permute-start(bf16[3,16,1024]{2,1,0:T(8,128)(2,1)S(1)} %get-tuple-element.9), channel_id=1, source_target_pairs={{0,4},{4,8},{8,12},{1,5},{5,9},{9,13},{2,6},{6,10},{10,14},{3,7},{... | collective-permute-start | bytes 294920 | tf_op jit(solution)/shard_map/ppermute | solution.py:210
  97.0 1.9 %collective-permute-start.1 = (bf16[3,16,1024]{2,1,0:T(8,128)(2,1)S(1)}, bf16[3,16,1024]{2,1,0:T(8,128)(2,1)S(1)}, u32[]{:S(2)}, u32[]{:S(2)}) collective-permute-start(bf16[3,16,1024]{2,1,0:T(8,128)(2,1)S(1)} %get-tuple-element.8), channel_id=1, source_target_pairs={{4,0},{8,4},{12,8},{5,1},{9,5},{13,9},{6,2},{10,6},{14,10},{7,3},{... | collective-permute-start | bytes 294920 | tf_op jit(solution)/shard_map/ppermute | solution.py:210
  98.9 0.0 copy-done.3
  98.9 0.2 reverse
  99.1 0.1 slice.42
  99.2 0.8 pad.8.taps_ref
  99.9 0.0 collective-permute-done.prev_ref
  99.9 2.9 %collective-permute-done.1.next_ref = bf16[3,16,1024]{2,1,0:T(8,128)(2,1)S(1)} collective-permute-done((bf16[3,16,1024]{2,1,0:T(8,128)(2,1)S(1)}, bf16[3,16,1024]{2,1,0:T(8,128)(2,1)S(1)}, u32[]{:S(2)}, u32[]{:S(2)}) %collective-permute-start.1) | collective-permute-done | bytes 98336 | tf_op jit(solution)/shard_map/ppermute | solution.py:210
  102.9 0.0 copy-done.4
  102.9 0.6 copy-done.6
  103.5 9.1 %signal.1 = bf16[3,128,768]{2,1,0:T(8,128)(2,1)} custom-call(bf16[3,128,1024]{2,1,0:T(8,128)(2,1)} %drift.1.main_ref, bf16[3,16,1024]{2,1,0:T(8,128)(2,1)} %copy-done.4, bf16[3,16,1024]{2,1,0:T(8,128)(2,1)} %copy-done.6, f32[3,21,512]{2,1,0:T(8,128)} %pad.8.taps_ref), custom_call_target="tpu_custom_call" | custom-call | flops 6341787648 | bytes 1572864 | tf_op jit(solution)/shard_map/signal/pallas_call | solution.py:316
  112.6 3.5 %grads.1 = bf16[512,384]{1,0:T(8,128)(2,1)} custom-call(s32[24]{0:T(128)} %reshape.28.blk_ref, s32[12]{0:T(128)} %reshape.29.count_ref, bf16[192,32,128]{2,1,0:T(8,128)(2,1)} %bitcast.9, bf16[4,192,128]{2,1,0:T(8,128)(2,1)} %bitcast.11), custom_call_target="tpu_custom_call" | custom-call | tf_op jit(solution)/shard_map/grads/pallas_call | solution.py:327
  (12 shorter events, 0.1 us)
Async XLA Ops:
  8.0 13.4 %copy-start.1 = (bf16[3,128,768]{2,1,0:T(8,128)(2,1)S(1)}, bf16[3,128,768]{2,1,0:T(8,128)(2,1)}, u32[]{:S(2)}) copy-start(bf16[3,128,768]{2,1,0:T(8,128)(2,1)} %param.13) | copy-start | bytes 1769476
  8.0 45.1 %reduce-scatter.2.cloned.1.call-start = ((), (), s32[]{:S(2)}) async-start(), calls=%async_computation.2 | async-start | bytes 327680 | tf_op jit(solution)/shard_map/reduce_scatter | solution.py:268
  15.1 97.5 %all-gather.2.cloned.1.call-start = ((), (), s32[]{:S(2)}) async-start(), calls=%async_computation.3 | async-start | bytes 1671168 | tf_op jit(solution)/shard_map/all_gather | solution.py:303
  16.1 8.5 %collective-permute-start.2 = (bf16[3,128,256]{2,1,0:T(8,128)(2,1)S(1)}, bf16[3,128,256]{2,1,0:T(8,128)(2,1)S(1)}, u32[]{:S(2)}, u32[]{:S(2)}) collective-permute-start(bf16[3,128,256]{2,1,0:T(8,128)(2,1)S(1)} %slice.35), channel_id=1, source_target_pairs={{1,0},{2,1},{3,2},{5,4},{6,5},{7,6},{9,8},{10,9},{11,10},{13,12},{... | collective-permute-start | bytes 589832 | tf_op jit(solution)/shard_map/ppermute | solution.py:210
  24.7 11.0 %copy-start.2 = (bf16[3,128,1024]{2,1,0:T(8,128)(2,1)}, bf16[3,128,1024]{2,1,0:T(8,128)(2,1)S(1)}, u32[]{:S(2)}) copy-start(bf16[3,128,1024]{2,1,0:T(8,128)(2,1)S(1)} %constant_dynamic-update-slice_fusion.main_ref) | copy-start | bytes 2359300
  24.7 7.2 %collective-permute-start.3 = (bf16[3,16,1024]{2,1,0:T(8,128)(2,1)S(1)}, bf16[3,16,1024]{2,1,0:T(8,128)(2,1)S(1)}, u32[]{:S(2)}, u32[]{:S(2)}) collective-permute-start(bf16[3,16,1024]{2,1,0:T(8,128)(2,1)S(1)} %get-tuple-element.7), channel_id=1, source_target_pairs={{0,4},{4,8},{8,12},{1,5},{5,9},{9,13},{2,6},{6,10},{10,14},{3,7},{... | collective-permute-start | bytes 294920 | tf_op jit(solution)/shard_map/ppermute | solution.py:210
  29.3 6.3 %collective-permute-start.4 = (bf16[3,16,1024]{2,1,0:T(8,128)(2,1)S(1)}, bf16[3,16,1024]{2,1,0:T(8,128)(2,1)S(1)}, u32[]{:S(2)}, u32[]{:S(2)}) collective-permute-start(bf16[3,16,1024]{2,1,0:T(8,128)(2,1)S(1)} %get-tuple-element.6), channel_id=1, source_target_pairs={{4,0},{8,4},{12,8},{5,1},{9,5},{13,9},{6,2},{10,6},{14,10},{7,3},{... | collective-permute-start | bytes 294920 | tf_op jit(solution)/shard_map/ppermute | solution.py:210
  31.9 3.8 %copy-start.5 = (bf16[3,16,1024]{2,1,0:T(8,128)(2,1)}, bf16[3,16,1024]{2,1,0:T(8,128)(2,1)S(1)}, u32[]{:S(2)}) copy-start(bf16[3,16,1024]{2,1,0:T(8,128)(2,1)S(1)} %collective-permute-done.3.prev_ref) | copy-start | bytes 294916
  35.7 0.6 copy-start.7
  48.3 33.4 %all-to-all-start = ((bf16[128,32,128]{2,1,0:T(8,128)(2,1)}), bf16[128,32,128]{2,1,0:T(8,128)(2,1)S(1)}, u32[]{:S(2)}, u32[]{:S(2)}) async-start(bf16[128,32,128]{2,1,0:T(8,128)(2,1)} %get-tuple-element.4), calls=%async_computation | async-start | bytes 2097152 | tf_op jit(solution)/shard_map/all_to_all | solution.py:267
  52.4 46.5 %copy-start.3 = (bf16[3,21,200]{2,1,0:T(8,128)(2,1)S(1)}, bf16[3,21,200]{2,1,0:T(8,128)(2,1)}, u32[]{:S(2)}) copy-start(bf16[3,21,200]{2,1,0:T(8,128)(2,1)} %param.12) | copy-start | bytes 75604
  81.7 1.0 copy-start
  94.1 5.8 %collective-permute-start = (bf16[3,16,1024]{2,1,0:T(8,128)(2,1)S(1)}, bf16[3,16,1024]{2,1,0:T(8,128)(2,1)S(1)}, u32[]{:S(2)}, u32[]{:S(2)}) collective-permute-start(bf16[3,16,1024]{2,1,0:T(8,128)(2,1)S(1)} %get-tuple-element.9), channel_id=1, source_target_pairs={{0,4},{4,8},{8,12},{1,5},{5,9},{9,13},{2,6},{6,10},{10,14},{3,7},{... | collective-permute-start | bytes 294920 | tf_op jit(solution)/shard_map/ppermute | solution.py:210
  97.0 5.9 %collective-permute-start.1 = (bf16[3,16,1024]{2,1,0:T(8,128)(2,1)S(1)}, bf16[3,16,1024]{2,1,0:T(8,128)(2,1)S(1)}, u32[]{:S(2)}, u32[]{:S(2)}) collective-permute-start(bf16[3,16,1024]{2,1,0:T(8,128)(2,1)S(1)} %get-tuple-element.8), channel_id=1, source_target_pairs={{4,0},{8,4},{12,8},{5,1},{9,5},{13,9},{6,2},{10,6},{14,10},{7,3},{... | collective-permute-start | bytes 294920 | tf_op jit(solution)/shard_map/ppermute | solution.py:210
  99.9 2.9 %copy-start.4 = (bf16[3,16,1024]{2,1,0:T(8,128)(2,1)}, bf16[3,16,1024]{2,1,0:T(8,128)(2,1)S(1)}, u32[]{:S(2)}) copy-start(bf16[3,16,1024]{2,1,0:T(8,128)(2,1)S(1)} %collective-permute-done.prev_ref) | copy-start | bytes 294916
  102.9 0.6 copy-start.6
Sparse Core Ops, SparseCore 0:
  15.2 20.7 reduce-scatter.1
Sparse Core Ops, SparseCore 1:
  48.4 46.2 all-gather.1
